TPU v7x, 256 devices: a whole 4x4x8 slice. The times are simulated.
256 devices in a mesh: gx: 8 (over y, core), gy: 4 (over z_lo), gz: 8 (over z_hi, x).
Axes of the slice: x: 4, y: 4, z: 8 (z_hi: 2, z_lo: 4; z = z_hi * 4 + z_lo), core: 2. Of those that a mesh axis runs over, the one named last changes fastest.
Arguments:
- tokens: bfloat16 [2048, 8192], P(('gx', 'gy'), 'gz'), may hold values from -6 to 6
- gate_weight: bfloat16 [8192, 28672], P('gz', ('gx', 'gy')), may hold values from -0.0625 to 0.0625
- up_weight: bfloat16 [8192, 28672], P('gz', ('gx', 'gy')), may hold values from -0.0625 to 0.0625
- down_weight: bfloat16 [28672, 8192], P(('gx', 'gy'), 'gz'), may hold values from -0.03125 to 0.03125
Outputs:
- layer_output: bfloat16 [2048, 8192], P(('gx', 'gy'), 'gz')
All inputs are finite; a program needn't handle non-finite values.
Results may differ from a plain program's by a relative error of at most 0.029.
Values may be sent and summed in bfloat16 or wider, within the bound.
A program may use at most 128 MiB of HBM per device.

v0:
```python
import jax
import jax.numpy as jnp
from jax import lax
from jax.sharding import PartitionSpec as P


def shards(tokens, gate_weight, up_weight, down_weight):
    gathered = lax.all_gather(tokens, "gx", axis=0, tiled=True)

    def column_product(weight_piece):
        return jnp.dot(gathered, weight_piece, preferred_element_type=jnp.float32)

    gate_partial = column_product(lax.all_gather(gate_weight, "gy", axis=1, tiled=True))
    up_partial = column_product(lax.all_gather(up_weight, "gy", axis=1, tiled=True))
    gate_sum, up_sum = (
        lax.psum_scatter(
            gate_partial.astype(jnp.bfloat16), "gz", scatter_dimension=0, tiled=True
        ).astype(jnp.float32),
        lax.psum_scatter(
            up_partial.astype(jnp.bfloat16), "gz", scatter_dimension=0, tiled=True
        ).astype(jnp.float32),
    )
    local_hidden = (jax.nn.silu(gate_sum) * up_sum).astype(jnp.bfloat16)
    hidden = lax.all_gather(local_hidden, "gz", axis=0, tiled=True)
    down_partial = jnp.dot(
        hidden,
        lax.all_gather(down_weight, "gy", axis=0, tiled=True),
        preferred_element_type=jnp.float32,
    )
    layer_output = lax.psum_scatter(
        down_partial.astype(jnp.bfloat16), "gx", scatter_dimension=0, tiled=True
    )
    return layer_output


def solution(mesh):
    return jax.shard_map(
        shards,
        mesh=mesh,
        in_specs=(
            P(("gx", "gy"), "gz"),
            P("gz", ("gx", "gy")),
            P("gz", ("gx", "gy")),
            P(("gx", "gy"), "gz"),
        ),
        out_specs=P(("gx", "gy"), "gz"),
        check_vma=False,
    )
```

profile of v0, /device:TPU:2, one launch (start us, length us, event | category | flops | bytes accessed | tf_op | source)
XLA Modules:
  0.0 839.3 jit_solution(120754620333667691)
XLA Ops:
  6.5 0.0 all-gather.6.cloned.1.call-start
  6.5 0.7 all-gather.6.cloned.1.call-update
  7.3 0.0 all-gather.8.cloned.1.call-start
  7.3 0.7 all-gather.8.cloned.1.call-update
  8.0 0.0 all-gather.10.cloned.1.call-start
  8.1 0.7 all-gather.10.cloned.1.call-update
  8.7 0.0 reduce-scatter.4.cloned.1.call-start
  8.8 29.3 %all-gather.6.cloned.1.call-done = bf16[512,1024]{1,0:T(8,128)(2,1)} async-done(((bf16[64,1024]{1,0:T(8,128)(2,1)}), bf16[512,1024]{1,0:T(8,128)(2,1)}) %all-gather.6.cloned.1.call-update) | async-done | bytes 1048592 | tf_op jit(solution)/shard_map/all_gather | solution.py:8
  38.1 0.0 copy-start
  38.1 137.6 %all-gather.8.cloned.1.call-done = bf16[1024,3584]{1,0:T(8,128)(2,1)} async-done(((bf16[1024,896]{1,0:T(8,128)(2,1)}), bf16[1024,3584]{1,0:T(8,128)(2,1)}) %all-gather.8.cloned.1.call-update) | async-done | bytes 7340048 | tf_op jit(solution)/shard_map/all_gather | solution.py:13
  175.7 9.2 %convolution_convert_fusion.1 = bf16[512,3584]{1,0:T(8,128)(2,1)} fusion(bf16[512,1024]{1,0:T(8,128)(2,1)} %all-gather.6.cloned.1.call-done, bf16[1024,3584]{1,0:T(8,128)(2,1)} %all-gather.8.cloned.1.call-done), kind=kOutput, calls=%fused_computation.1 | convolution fusion | flops 3759931392 | bytes 12058624 | tf_op jit(solution)/shard_map/dot_general | solution.py:11
  184.9 0.0 reduce-scatter.4.cloned.1.call-update
  184.9 0.0 reduce-scatter.6.cloned.1.call-start
  185.0 128.1 %all-gather.10.cloned.1.call-done = bf16[1024,3584]{1,0:T(8,128)(2,1)} async-done(((bf16[1024,896]{1,0:T(8,128)(2,1)}), bf16[1024,3584]{1,0:T(8,128)(2,1)}) %all-gather.10.cloned.1.call-update) | async-done | bytes 7340048 | tf_op jit(solution)/shard_map/all_gather | solution.py:14
  313.1 0.0 copy-done
  313.1 8.4 %convolution_convert_fusion = bf16[512,3584]{1,0:T(8,128)(2,1)} fusion(bf16[512,1024]{1,0:T(8,128)(2,1)S(1)} %copy-done, bf16[1024,3584]{1,0:T(8,128)(2,1)} %all-gather.10.cloned.1.call-done), kind=kOutput, calls=%fused_computation | convolution fusion | flops 3759931392 | bytes 12058624 | tf_op jit(solution)/shard_map/dot_general | solution.py:11
  321.5 0.0 reduce-scatter.6.cloned.1.call-update
  321.6 0.0 all-gather.14.cloned.1.call-start
  321.6 0.5 all-gather.14.cloned.1.call-update
  322.1 0.0 all-gather.12.cloned.1.call-start
  322.2 115.4 %reduce-scatter.4.cloned.1.call-done = bf16[64,3584]{1,0:T(8,128)(2,1)} async-done(((bf16[512,3584]{1,0:T(8,128)(2,1)}), bf16[64,3584]{1,0:T(8,128)(2,1)}) %reduce-scatter.4.cloned.1.call-update) | async-done | bytes 458768 | tf_op jit(solution)/shard_map/reduce_scatter | solution.py:16
  437.6 121.3 %reduce-scatter.6.cloned.1.call-done = bf16[64,3584]{1,0:T(8,128)(2,1)} async-done(((bf16[512,3584]{1,0:T(8,128)(2,1)}), bf16[64,3584]{1,0:T(8,128)(2,1)}) %reduce-scatter.6.cloned.1.call-update) | async-done | bytes 458768 | tf_op jit(solution)/shard_map/reduce_scatter | solution.py:19
  558.9 2.2 fusion.4
  561.1 0.0 all-gather.12.cloned.1.call-update
  561.1 0.0 reduce-scatter.8.cloned.1.call-start
  561.2 131.1 %all-gather.14.cloned.1.call-done = bf16[3584,1024]{1,0:T(8,128)(2,1)} async-done(((bf16[896,1024]{1,0:T(8,128)(2,1)}), bf16[3584,1024]{1,0:T(8,128)(2,1)}) %all-gather.14.cloned.1.call-update) | async-done | bytes 7340048 | tf_op jit(solution)/shard_map/all_gather | solution.py:27
  692.3 100.6 %all-gather.12.cloned.1.call-done = bf16[512,3584]{1,0:T(8,128)(2,1)} async-done(((bf16[64,3584]{1,0:T(8,128)(2,1)}), bf16[512,3584]{1,0:T(8,128)(2,1)}) %all-gather.12.cloned.1.call-update) | async-done | bytes 3670032 | tf_op jit(solution)/shard_map/all_gather | solution.py:24
  792.9 9.1 %convolution_convert_fusion.2 = bf16[512,1024]{1,0:T(8,128)(2,1)} fusion(bf16[512,3584]{1,0:T(8,128)(2,1)} %all-gather.12.cloned.1.call-done, bf16[3584,1024]{1,0:T(8,128)(2,1)} %all-gather.14.cloned.1.call-done), kind=kOutput, calls=%fused_computation.2 | convolution fusion | flops 3758620672 | bytes 12058624 | tf_op jit(solution)/shard_map/dot_general | solution.py:25
  802.0 0.0 reduce-scatter.8.cloned.1.call-update
  802.0 30.5 %reduce-scatter.8.cloned.1.call-done = bf16[64,1024]{1,0:T(8,128)(2,1)} async-done(((bf16[512,1024]{1,0:T(8,128)(2,1)}), bf16[64,1024]{1,0:T(8,128)(2,1)}) %reduce-scatter.8.cloned.1.call-update) | async-done | bytes 131088 | tf_op jit(solution)/shard_map/reduce_scatter | solution.py:30
Async XLA Ops:
  6.5 31.6 %all-gather.6.cloned.1.call-start = ((), (), s32[]{:S(2)}) async-start(), calls=%async_computation.3 | async-start | bytes 1179648 | tf_op jit(solution)/shard_map/all_gather | solution.py:8
  7.3 168.4 %all-gather.8.cloned.1.call-start = ((), (), s32[]{:S(2)}) async-start(), calls=%async_computation.4 | async-start | bytes 9175040 | tf_op jit(solution)/shard_map/all_gather | solution.py:13
  8.0 305.1 %all-gather.10.cloned.1.call-start = ((), (), s32[]{:S(2)}) async-start(), calls=%async_computation.6 | async-start | bytes 9175040 | tf_op jit(solution)/shard_map/all_gather | solution.py:14
  8.7 428.9 %reduce-scatter.4.cloned.1.call-start = ((), (), s32[]{:S(2)}) async-start(), calls=%async_computation.5 | async-start | bytes 4128768 | tf_op jit(solution)/shard_map/reduce_scatter | solution.py:16
  38.1 275.0 %copy-start = (bf16[512,1024]{1,0:T(8,128)(2,1)S(1)}, bf16[512,1024]{1,0:T(8,128)(2,1)}, u32[]{:S(2)}) copy-start(bf16[512,1024]{1,0:T(8,128)(2,1)} %all-gather.6.cloned.1.call-done) | copy-start | bytes 3145732
  184.9 374.0 %reduce-scatter.6.cloned.1.call-start = ((), (), s32[]{:S(2)}) async-start(), calls=%async_computation.7 | async-start | bytes 4128768 | tf_op jit(solution)/shard_map/reduce_scatter | solution.py:19
  321.6 370.7 %all-gather.14.cloned.1.call-start = ((), (), s32[]{:S(2)}) async-start(), calls=%async_computation.9 | async-start | bytes 9175040 | tf_op jit(solution)/shard_map/all_gather | solution.py:27
  322.1 470.7 %all-gather.12.cloned.1.call-start = ((), (), s32[]{:S(2)}) async-start(), calls=%async_computation.8 | async-start | bytes 4128768 | tf_op jit(solution)/shard_map/all_gather | solution.py:24
  561.1 271.4 %reduce-scatter.8.cloned.1.call-start = ((), (), s32[]{:S(2)}) async-start(), calls=%async_computation.10 | async-start | bytes 1179648 | tf_op jit(solution)/shard_map/reduce_scatter | solution.py:30
Sparse Core Ops, SparseCore 0:
  9.2 28.8 all-gather.5
  40.0 135.6 all-gather.7
  177.5 135.5 all-gather.9
  317.2 120.3 reduce-scatter.3
  442.3 116.5 reduce-scatter.5
  560.6 131.6 all-gather.13
  694.9 97.9 all-gather.11
  802.1 30.3 reduce-scatter.7
where the time goes:
time: 839 us
  waiting for transfers between devices  797 us (95%)
  matrix products  26.8 us (3%)
  between operations  13.5 us (2%)
    all_gather x1, waiting for transfers between devices, shards(): lax.all_gather(gate_weight, 'gy', axis=1, tiled=True)  138 us
    all_gather x1, waiting for transfers between devices, shards(): lax.all_gather(down_weight, 'gy', axis=0, tiled=True)  131 us
    all_gather x1, waiting for transfers between devices, shards(): lax.all_gather(up_weight, 'gy', axis=1, tiled=True)  128 us
    reduce_scatter x1, waiting for transfers between devices, shards(): lax.psum_scatter(up_partial.astype(jnp.bfloat16), 'gz', scatter_dimension...  121 us
    reduce_scatter x1, waiting for transfers between devices, shards(): lax.psum_scatter(gate_partial.astype(jnp.bfloat16), 'gz', scatter_dimensi...  115 us
    all_gather x1, waiting for transfers between devices, shards(): hidden = lax.all_gather(local_hidden, 'gz', axis=0, tiled=True)  101 us
    reduce_scatter x1, waiting for transfers between devices, shards(): lax.psum_scatter(down_partial.astype(jnp.bfloat16), 'gx', scatter_dimensi...  30.5 us
    all_gather x1, waiting for transfers between devices, shards(): gathered = lax.all_gather(tokens, 'gx', axis=0, tiled=True)  29.3 us
  transfers between devices with their start and end apart: 8, of which 8 were waited for; matrix products, arithmetic and copies ran while one was open for 2% of the time, Pallas kernels for 0%

commit v1 on v0

--- a/solution.py
+++ b/solution.py
@@ -24,7 +24,9 @@
     hidden = lax.all_gather(local_hidden, "gz", axis=0, tiled=True)
     down_partial = jnp.dot(
         hidden,
-        lax.all_gather(down_weight, "gy", axis=0, tiled=True),
+        jnp.concatenate(
+            lax.all_to_all(jnp.stack([down_weight] * lax.axis_size("gy")), "gy", 0, 0), axis=0
+        ),
         preferred_element_type=jnp.float32,
     )
     layer_output = lax.psum_scatter(

time: 839 us -> 787 us (0.938)
  waiting for transfers between devices: 797 us -> 734 us
    all_gather x1 -> x0, waiting for transfers between devices: 131 us -> none  [shards(): lax.all_gather(down_weight, 'gy', axis=0, tiled=True)]
    reduce_scatter x1, waiting for transfers between devices: 115 us -> 164 us  [shards(): lax.psum_scatter(gate_partial.astype(jnp.bfloat16), 'gz', scatter_dimensi...]
    reduce_scatter x1, waiting for transfers between devices: 121 us -> 149 us  [shards(): lax.psum_scatter(up_partial.astype(jnp.bfloat16), 'gz', scatter_dimension...]
  transfers between devices with their start and end apart: 8 -> 8, of which waited for: 8 -> 7; matrix products, arithmetic and copies ran while one was open for 2% -> 3% of each run, Pallas kernels for 0% -> 0%
where the time goes in v1:
time: 787 us
  waiting for transfers between devices  734 us (93%)
  matrix products  26.9 us (3%)
  between operations  13.5 us (2%)
    reduce_scatter x1, waiting for transfers between devices, shards(): lax.psum_scatter(gate_partial.astype(jnp.bfloat16), 'gz', scatter_dimensi...  164 us
    reduce_scatter x1, waiting for transfers between devices, shards(): lax.psum_scatter(up_partial.astype(jnp.bfloat16), 'gz', scatter_dimension...  149 us
    all_gather x1, waiting for transfers between devices, shards(): lax.all_gather(gate_weight, 'gy', axis=1, tiled=True)  138 us
    all_gather x1, waiting for transfers between devices, shards(): lax.all_gather(up_weight, 'gy', axis=1, tiled=True)  128 us
    all_gather x1, waiting for transfers between devices, shards(): hidden = lax.all_gather(local_hidden, 'gz', axis=0, tiled=True)  94.3 us
    reduce_scatter x1, waiting for transfers between devices, shards(): lax.psum_scatter(down_partial.astype(jnp.bfloat16), 'gx', scatter_dimensi...  30.5 us
    all_gather x1, waiting for transfers between devices, shards(): gathered = lax.all_gather(tokens, 'gx', axis=0, tiled=True)  29.3 us
    dot_general x2, matrix products, column_product(): return jnp.dot(gathered, weight_piece, preferred_element_type=jnp.float32)  17.7 us
  transfers between devices with their start and end apart: 8, of which 7 were waited for; matrix products, arithmetic and copies ran while one was open for 3% of the time, Pallas kernels for 0%

profile of v1, /device:TPU:2, one launch (start us, length us, event | category | flops | bytes accessed | tf_op | source)
XLA Modules:
  0.0 786.6 jit_solution(17991095188411551644)
XLA Ops:
  6.5 0.0 all-gather.5.cloned.1.call-start
  6.5 0.7 all-gather.5.cloned.1.call-update
  7.3 0.0 all-gather.7.cloned.1.call-start
  7.3 0.7 all-gather.7.cloned.1.call-update
  8.0 0.0 all-gather.9.cloned.1.call-start
  8.1 0.7 all-gather.9.cloned.1.call-update
  8.7 0.0 reduce-scatter.4.cloned.1.call-start
  8.8 29.3 %all-gather.5.cloned.1.call-done = bf16[512,1024]{1,0:T(8,128)(2,1)} async-done(((bf16[64,1024]{1,0:T(8,128)(2,1)}), bf16[512,1024]{1,0:T(8,128)(2,1)}) %all-gather.5.cloned.1.call-update) | async-done | bytes 1048592 | tf_op jit(solution)/shard_map/all_gather | solution.py:8
  38.1 0.0 copy-start.1
  38.1 137.6 %all-gather.7.cloned.1.call-done = bf16[1024,3584]{1,0:T(8,128)(2,1)} async-done(((bf16[1024,896]{1,0:T(8,128)(2,1)}), bf16[1024,3584]{1,0:T(8,128)(2,1)}) %all-gather.7.cloned.1.call-update) | async-done | bytes 7340048 | tf_op jit(solution)/shard_map/all_gather | solution.py:13
  175.7 9.2 %convolution_convert_fusion.1 = bf16[512,3584]{1,0:T(8,128)(2,1)} fusion(bf16[512,1024]{1,0:T(8,128)(2,1)} %all-gather.5.cloned.1.call-done, bf16[1024,3584]{1,0:T(8,128)(2,1)} %all-gather.7.cloned.1.call-done), kind=kOutput, calls=%fused_computation.1 | convolution fusion | flops 3759931392 | bytes 12058624 | tf_op jit(solution)/shard_map/dot_general | solution.py:11
  184.9 0.0 reduce-scatter.4.cloned.1.call-update
  184.9 0.0 copy-start
  184.9 0.0 reduce-scatter.6.cloned.1.call-start
  185.0 128.1 %all-gather.9.cloned.1.call-done = bf16[1024,3584]{1,0:T(8,128)(2,1)} async-done(((bf16[1024,896]{1,0:T(8,128)(2,1)}), bf16[1024,3584]{1,0:T(8,128)(2,1)}) %all-gather.9.cloned.1.call-update) | async-done | bytes 7340048 | tf_op jit(solution)/shard_map/all_gather | solution.py:14
  313.1 0.0 copy-done.1
  313.1 8.5 %convolution_convert_fusion = bf16[512,3584]{1,0:T(8,128)(2,1)} fusion(bf16[512,1024]{1,0:T(8,128)(2,1)S(1)} %copy-done.1, bf16[1024,3584]{1,0:T(8,128)(2,1)} %all-gather.9.cloned.1.call-done), kind=kOutput, calls=%fused_computation | convolution fusion | flops 3759931392 | bytes 12058624 | tf_op jit(solution)/shard_map/dot_general | solution.py:11
  321.6 0.0 reduce-scatter.6.cloned.1.call-update
  321.6 0.0 copy-done
  321.6 4.0 stack.2
  325.6 5.5 all-to-all-start
  331.1 0.0 all-gather.11.cloned.1.call-start
  331.1 163.7 %reduce-scatter.4.cloned.1.call-done = bf16[64,3584]{1,0:T(8,128)(2,1)} async-done(((bf16[512,3584]{1,0:T(8,128)(2,1)}), bf16[64,3584]{1,0:T(8,128)(2,1)}) %reduce-scatter.4.cloned.1.call-update) | async-done | bytes 458768 | tf_op jit(solution)/shard_map/reduce_scatter | solution.py:16
  494.8 148.7 %reduce-scatter.6.cloned.1.call-done = bf16[64,3584]{1,0:T(8,128)(2,1)} async-done(((bf16[512,3584]{1,0:T(8,128)(2,1)}), bf16[64,3584]{1,0:T(8,128)(2,1)}) %reduce-scatter.6.cloned.1.call-update) | async-done | bytes 458768 | tf_op jit(solution)/shard_map/reduce_scatter | solution.py:19
  643.6 2.2 fusion.4
  645.8 0.0 all-gather.11.cloned.1.call-update
  645.8 0.0 reduce-scatter.8.cloned.1.call-start
  645.8 0.0 all-to-all-done
  645.8 94.3 %all-gather.11.cloned.1.call-done = bf16[512,3584]{1,0:T(8,128)(2,1)} async-done(((bf16[64,3584]{1,0:T(8,128)(2,1)}), bf16[512,3584]{1,0:T(8,128)(2,1)}) %all-gather.11.cloned.1.call-update) | async-done | bytes 3670032 | tf_op jit(solution)/shard_map/all_gather | solution.py:24
  740.1 9.2 %convolution_convert_fusion.2 = bf16[512,1024]{1,0:T(8,128)(2,1)} fusion(bf16[512,3584]{1,0:T(8,128)(2,1)} %all-gather.11.cloned.1.call-done, bf16[3584,1024]{1,0:T(8,128)(2,1)} %bitcast), kind=kOutput, calls=%fused_computation.2 | convolution fusion | flops 3758620672 | bytes 12058624 | tf_op jit(solution)/shard_map/dot_general | solution.py:25
  749.3 0.0 reduce-scatter.8.cloned.1.call-update
  749.3 30.5 %reduce-scatter.8.cloned.1.call-done = bf16[64,1024]{1,0:T(8,128)(2,1)} async-done(((bf16[512,1024]{1,0:T(8,128)(2,1)}), bf16[64,1024]{1,0:T(8,128)(2,1)}) %reduce-scatter.8.cloned.1.call-update) | async-done | bytes 131088 | tf_op jit(solution)/shard_map/reduce_scatter | solution.py:32
Async XLA Ops:
  6.5 31.6 %all-gather.5.cloned.1.call-start = ((), (), s32[]{:S(2)}) async-start(), calls=%async_computation.4 | async-start | bytes 1179648 | tf_op jit(solution)/shard_map/all_gather | solution.py:8
  7.3 168.4 %all-gather.7.cloned.1.call-start = ((), (), s32[]{:S(2)}) async-start(), calls=%async_computation.5 | async-start | bytes 9175040 | tf_op jit(solution)/shard_map/all_gather | solution.py:13
  8.0 305.1 %all-gather.9.cloned.1.call-start = ((), (), s32[]{:S(2)}) async-start(), calls=%async_computation.7 | async-start | bytes 9175040 | tf_op jit(solution)/shard_map/all_gather | solution.py:14
  8.7 486.1 %reduce-scatter.4.cloned.1.call-start = ((), (), s32[]{:S(2)}) async-start(), calls=%async_computation.6 | async-start | bytes 4128768 | tf_op jit(solution)/shard_map/reduce_scatter | solution.py:16
  38.1 275.0 %copy-start.1 = (bf16[512,1024]{1,0:T(8,128)(2,1)S(1)}, bf16[512,1024]{1,0:T(8,128)(2,1)}, u32[]{:S(2)}) copy-start(bf16[512,1024]{1,0:T(8,128)(2,1)} %all-gather.5.cloned.1.call-done) | copy-start | bytes 3145732
  184.9 136.7 %copy-start = (bf16[896,1024]{1,0:T(8,128)(2,1)S(1)}, bf16[896,1024]{1,0:T(8,128)(2,1)}, u32[]{:S(2)}) copy-start(bf16[896,1024]{1,0:T(8,128)(2,1)} %param.7) | copy-start | bytes 5505028
  184.9 458.6 %reduce-scatter.6.cloned.1.call-start = ((), (), s32[]{:S(2)}) async-start(), calls=%async_computation.8 | async-start | bytes 4128768 | tf_op jit(solution)/shard_map/reduce_scatter | solution.py:19
  325.6 320.3 %all-to-all-start = ((bf16[4,896,1024]{2,1,0:T(8,128)(2,1)}), bf16[4,896,1024]{2,1,0:T(8,128)(2,1)}, u32[]{:S(2)}, u32[]{:S(2)}) async-start(bf16[4,896,1024]{2,1,0:T(8,128)(2,1)} %stack.2), calls=%async_computation.2 | async-start | bytes 14680064 | tf_op jit(solution)/shard_map/all_to_all | solution.py:28
  331.1 409.0 %all-gather.11.cloned.1.call-start = ((), (), s32[]{:S(2)}) async-start(), calls=%async_computation.9 | async-start | bytes 4128768 | tf_op jit(solution)/shard_map/all_gather | solution.py:24
  645.8 134.0 %reduce-scatter.8.cloned.1.call-start = ((), (), s32[]{:S(2)}) async-start(), calls=%async_computation.10 | async-start | bytes 1179648 | tf_op jit(solution)/shard_map/reduce_scatter | solution.py:32
Sparse Core Ops, SparseCore 0:
  9.2 28.8 all-gather.4
  40.0 135.6 all-gather.6
  177.5 135.5 all-gather.8
  317.2 177.5 reduce-scatter.3
  499.5 143.9 reduce-scatter.5
  646.0 94.0 all-gather.10
  749.4 30.3 reduce-scatter.7
